TPU v7x, 32 devices: a whole 2x2x4 slice. The times are simulated.
32 devices in a mesh: sec: 2 (over x), blk: 8 (over z, y), mp: 2 (over core).
Axes of the slice: x: 2, y: 2, z: 4, core: 2. Of those that a mesh axis runs over, the one named last changes fastest.
Arguments:
- image_pooled: bfloat16 [1536, 1536], P('blk', ('sec', 'mp')), may hold values from -4 to 4
- text_pooled: bfloat16 [1536, 2048], P('blk', ('sec', 'mp')), may hold values from -4 to 4
- image_proj: bfloat16 [1536, 1152], P(('sec', 'mp')), may hold values from -0.15625 to 0.15625
- text_proj: bfloat16 [2048, 1152], P(('sec', 'mp')), may hold values from -0.125 to 0.125
- natural_log_multiplier: float32 [1], replicated, may hold values from 1.4 to 2.3
- logit_bias: float32 [1], replicated, may hold values from -2 to -0.5
- match_cluster_labels: int32 [1536], P('blk'), may hold values from 0 to 1535
Outputs:
- pair_loss: float32 [2, 1536], P('sec', 'blk')
- image_grad: bfloat16 [1536, 1536], P('blk', ('sec', 'mp'))
- text_grad: bfloat16 [1536, 2048], P('blk', ('sec', 'mp'))
All inputs are finite; a program needn't handle non-finite values.
Results may differ from a plain program's by a relative error of at most 0.0065.
Values may be sent and summed in bfloat16 or wider, within the bound.
No kernel may reach another device: no remote copies, remote signals or barrier semaphores. Data moves between devices by JAX's collectives and lax.ppermute only.
A program may use at most 128 MiB of HBM per device.

v0:
```python
import jax
import jax.numpy as jnp
from jax import lax
from jax.sharding import PartitionSpec as P


def unit_rows(embedding):
    row_norm = jnp.sqrt(jnp.sum(embedding * embedding, axis=1, keepdims=True) + 1e-06)
    return (embedding / row_norm, row_norm)


def per_device(
    image_pooled,
    text_pooled,
    image_proj,
    text_proj,
    natural_log_multiplier,
    logit_bias,
    match_cluster_labels,
):
    part_image = jnp.dot(image_pooled, image_proj, preferred_element_type=jnp.float32)
    part_text = jnp.dot(text_pooled, text_proj, preferred_element_type=jnp.float32)
    stacked = jnp.stack([part_image, part_text])
    section = lax.axis_index("sec")
    both_sums = lax.psum(stacked, ("sec", "mp"))
    own_emb = lax.dynamic_index_in_dim(both_sums, section, 0, keepdims=False)
    other_emb = lax.dynamic_index_in_dim(both_sums, 1 - section, 0, keepdims=False)
    own_unit, own_norm = unit_rows(own_emb)
    resident_slice = own_unit.astype(jnp.bfloat16)
    other_unit, other_norm = unit_rows(other_emb)
    counterpart_slice = other_unit.astype(jnp.bfloat16)
    sharpness_factor = jnp.exp(natural_log_multiplier[0])
    shift_quantity = logit_bias[0]
    visit_rows = lax.all_gather(counterpart_slice, "blk", axis=0, tiled=True)
    visited_ids = lax.all_gather(match_cluster_labels, "blk", axis=0, tiled=True)
    agreement_scores_matrix = (
        sharpness_factor
        * lax.dot_general(
            resident_slice, visit_rows, (((1,), (1,)), ((), ())), preferred_element_type=jnp.float32
        )
        + shift_quantity
    )
    desired_polarity = jnp.where(
        match_cluster_labels[:, None] == visited_ids[None, :], 1.0, -1.0
    ).astype(jnp.float32)
    row_losses = jnp.sum(jax.nn.softplus(-desired_polarity * agreement_scores_matrix), axis=1)
    penalty_factor = (
        -sharpness_factor
        * desired_polarity
        * jax.nn.sigmoid(-desired_polarity * agreement_scores_matrix)
    ).astype(jnp.bfloat16)
    unit_grad = jnp.dot(penalty_factor, visit_rows, preferred_element_type=jnp.float32)
    unit_grad, row_losses = (unit_grad, row_losses)
    projection = jnp.sum(own_unit * unit_grad, axis=1, keepdims=True)
    own_demb = ((unit_grad - own_unit * projection) / own_norm).astype(jnp.bfloat16)
    both_grads = lax.all_gather(own_demb[None], "sec", axis=0, tiled=True)
    image_grad = lax.dot_general(
        both_grads[0], image_proj, (((1,), (1,)), ((), ())), preferred_element_type=jnp.float32
    ).astype(jnp.bfloat16)
    text_grad = lax.dot_general(
        both_grads[1], text_proj, (((1,), (1,)), ((), ())), preferred_element_type=jnp.float32
    ).astype(jnp.bfloat16)
    return (row_losses[None, :], image_grad, text_grad)


def solution(mesh):
    placed = (
        P("blk", ("sec", "mp")),
        P("blk", ("sec", "mp")),
        P(("sec", "mp"), None),
        P(("sec", "mp"), None),
        P(),
        P(),
        P("blk"),
    )
    return jax.shard_map(
        per_device,
        mesh=mesh,
        in_specs=placed,
        out_specs=(P("sec", "blk"), P("blk", ("sec", "mp")), P("blk", ("sec", "mp"))),
        check_vma=False,
    )
```

profile of v0, /device:TPU:0, one launch (start us, length us, event | category | flops | bytes accessed | tf_op | source)
XLA Modules:
  0.0 155.9 jit_solution(17890607806463199969)
XLA Ops:
  7.2 0.0 copy-start
  7.2 0.0 copy-start.4
  7.2 0.0 copy-start.2
  7.2 0.0 all-reduce.3.cloned.1.call-start
  7.2 1.2 copy-done
  8.4 1.4 convolution_bitcast_fusion
  9.8 0.0 copy-done.4
  9.8 0.0 copy-done.2
  9.8 0.4 convolution_bitcast_fusion.1
  10.2 1.3 pad_maximum_fusion
  11.6 0.0 all-reduce.3.cloned.1.call-update
  11.6 0.0 all-gather.3.cloned.1.call-start
  11.6 48.8 %all-reduce.3.cloned.1.call-done = f32[2,192,1152]{2,1,0:T(8,128)} async-done(((f32[2,192,1152]{2,1,0:T(8,128)}), f32[2,192,1152]{2,1,0:T(8,128)}) %all-reduce.3.cloned.1.call-update) | async-done | bytes 1769488 | tf_op jit(solution)/shard_map/psum | solution.py:25
  60.5 0.0 copy-start.1
  60.5 1.8 %fusion.7 = (f32[192]{0:T(256)S(1)}, f32[192]{0:T(256)S(1)}) fusion(f32[2,192,1152]{2,1,0:T(8,128)} %all-reduce.3.cloned.1.call-done, s32[]{:T(128)S(6)} %select_n.16, s32[]{:T(128)S(6)} %select_n.17), kind=kLoop, calls=%fused_computation.20 | loop fusion | flops 884352 | bytes 1771016 | tf_op jit(solution)/shard_map/reduce_sum | solution.py:8
  62.2 0.0 copy-start.7
  62.3 0.0 copy-start.5
  62.3 0.2 copy-done.1
  62.5 0.9 fusion.6
  63.4 0.0 all-gather.3.cloned.1.call-update
  64.7 0.0 copy-done.7
  64.8 0.6 dynamic-slice
  66.0 0.0 copy-done.5
  66.0 0.3 dynamic-update-slice
  66.3 12.1 %all-reduce = s32[1536]{0:T(1024)S(1)} all-reduce(s32[1536]{0:T(1024)S(1)} %dynamic-update-slice), channel_id=1, replica_groups=mesh['sec'=2,'blk'=8,'mp'=2] {'blk'}, use_global_device_ids=true, to_apply=%add | all-reduce | flops 1536 | bytes 12288
  78.4 50.5 %all-gather.3.cloned.1.call-done = bf16[1536,1152]{1,0:T(8,128)(2,1)} async-done(((bf16[192,1152]{1,0:T(8,128)(2,1)}), bf16[1536,1152]{1,0:T(8,128)(2,1)}) %all-gather.3.cloned.1.call-update) | async-done | bytes 3538960 | tf_op jit(solution)/shard_map/all_gather | solution.py:34
  128.9 0.0 copy-start.6
  128.9 4.7 %fusion.4 = (f32[192]{0:T(256)}, f32[192,1536]{1,0:T(8,128)S(1)}) fusion(f32[]{:T(128)} %bitcast.37, bf16[1536,1152]{1,0:T(8,128)(2,1)} %all-gather.3.cloned.1.call-done, f32[192]{0:T(256)S(1)} %add_sqrt_fusion.1, f32[2,192,1152]{2,1,0:T(8,128)S(1)} %copy-done.1, s32[]{:T(128)S(6)} %select_n.16, f32[]{:T(128)} %bitcast.1, s32[1536]{0:T(1024)S(1)} %all-reduce, ...), kind=kOutput, calls=%fused_computation.11 | convolution fusion | flops 683753280 | bytes 5614348 | tf_op jit(solution)/shard_map/dot_general | solution.py:38
  133.6 0.0 copy-done.6
  133.6 1.1 multiply_reduce_fusion
  134.7 0.2 divide_convert_fusion
  135.0 0.0 copy-start.3
  135.0 11.7 %all-gather = bf16[384,1152]{1,0:T(8,128)(2,1)S(1)} all-gather(bf16[192,1152]{1,0:T(8,128)(2,1)S(1)} %divide_convert_fusion), channel_id=2, replica_groups=mesh['sec'=2,'blk'=8,'mp'=2] {'sec'}, dimensions={0}, use_global_device_ids=true | all-gather | bytes 1327104 | tf_op jit(solution)/shard_map/all_gather | solution.py:56
  146.7 0.0 copy-done.3
  146.7 1.1 convolution_convert_fusion.1
  147.8 1.2 convolution_convert_fusion
  (3 shorter events, 0.0 us)
Async XLA Ops:
  7.2 1.3 copy-start
  7.2 2.6 %copy-start.4 = (bf16[192,384]{1,0:T(8,128)(2,1)S(1)}, bf16[192,384]{1,0:T(8,128)(2,1)}, u32[]{:S(2)}) copy-start(bf16[192,384]{1,0:T(8,128)(2,1)} %param.7) | copy-start | bytes 442372
  7.2 2.6 %copy-start.2 = (bf16[384,1152]{1,0:T(8,128)(2,1)S(1)}, bf16[384,1152]{1,0:T(8,128)(2,1)}, u32[]{:S(2)}) copy-start(bf16[384,1152]{1,0:T(8,128)(2,1)} %param.9) | copy-start | bytes 2654212
  7.2 53.3 %all-reduce.3.cloned.1.call-start = ((), (), s32[]{:S(2)}) async-start(), calls=%async_computation | async-start | bytes 3538944 | tf_op jit(solution)/shard_map/psum | solution.py:25
  11.6 117.3 %all-gather.3.cloned.1.call-start = ((), (), s32[]{:S(2)}) async-start(), calls=%async_computation.1 | async-start | bytes 3981312 | tf_op jit(solution)/shard_map/all_gather | solution.py:34
  60.5 2.0 %copy-start.1 = (f32[2,192,1152]{2,1,0:T(8,128)S(1)}, f32[2,192,1152]{2,1,0:T(8,128)}, u32[]{:S(2)}) copy-start(f32[2,192,1152]{2,1,0:T(8,128)} %all-reduce.3.cloned.1.call-done) | copy-start | bytes 5308420
  62.2 2.5 %copy-start.7 = (u32[32]{0:T(128)S(1)}, u32[32]{0:T(128)}, u32[]{:S(2)}) copy-start(u32[32]{0:T(128)} %constant.31) | copy-start | bytes 388
  62.3 3.8 %copy-start.5 = (s32[192]{0:T(256)S(1)}, s32[192]{0:T(256)}, u32[]{:S(2)}) copy-start(s32[192]{0:T(256)} %param.13) | copy-start | bytes 2308
  128.9 4.7 %copy-start.6 = (bf16[1536,1152]{1,0:T(8,128)(2,1)S(1)}, bf16[1536,1152]{1,0:T(8,128)(2,1)}, u32[]{:S(2)}) copy-start(bf16[1536,1152]{1,0:T(8,128)(2,1)} %all-gather.3.cloned.1.call-done) | copy-start | bytes 10616836
  135.0 11.8 %copy-start.3 = (bf16[384,1152]{1,0:T(8,128)(2,1)S(1)}, bf16[384,1152]{1,0:T(8,128)(2,1)}, u32[]{:S(2)}) copy-start(bf16[384,1152]{1,0:T(8,128)(2,1)} %param.9) | copy-start | bytes 2654212
Sparse Core Ops, SparseCore 0:
  11.7 48.7 all-reduce.2
  63.5 65.3 all-gather.2
where the time goes:
time: 156 us
  waiting for transfers between devices  99.4 us (64%)
  blocking collectives  23.8 us (15%)
  between operations  16.2 us (10%)
  matrix products  9.9 us (6%)
  other arithmetic  4.2 us (3%)
  local copies, waits for them, and re-layouts  2.31 us (1%)
    all_gather x1, waiting for transfers between devices, per_device(): visit_rows = lax.all_gather(counterpart_slice, 'blk', axis=0, tiled=True)  50.5 us
    psum x1, waiting for transfers between devices, per_device(): both_sums = lax.psum(stacked, ('sec', 'mp'))  48.8 us
    unnamed x1, blocking collectives  12.1 us
    all_gather x1, blocking collectives, per_device(): both_grads = lax.all_gather(own_demb[None], 'sec', axis=0, tiled=True)  11.7 us
    dot_general x1, matrix products, per_device(): lax.dot_general(resident_slice, visit_rows, (((1,), (1,)), ((), ())), pre...  4.68 us
  transfers between devices with their start and end apart: 2, of which 2 were waited for; matrix products, arithmetic and copies ran while one was open for 1% of the time, Pallas kernels for 0%

commit v1 on v0

--- a/solution.py
+++ b/solution.py
@@ -22,7 +22,8 @@
     part_text = jnp.dot(text_pooled, text_proj, preferred_element_type=jnp.float32)
     stacked = jnp.stack([part_image, part_text])
     section = lax.axis_index("sec")
-    both_sums = lax.psum(stacked, ("sec", "mp"))
+    partial = lax.psum(stacked, "mp")
+    both_sums = lax.psum(partial, "sec")
     own_emb = lax.dynamic_index_in_dim(both_sums, section, 0, keepdims=False)
     other_emb = lax.dynamic_index_in_dim(both_sums, 1 - section, 0, keepdims=False)
     own_unit, own_norm = unit_rows(own_emb)

time: 156 us -> 190 us (1.22)
  waiting for transfers between devices: 99.4 us -> 133 us
    psum x1 -> x2, waiting for transfers between devices: 48.8 us -> 82.8 us  [the longest x1 59.3 us: per_device(): both_sums = lax.psum(partial, 'sec')]
  transfers between devices with their start and end apart: 2 -> 3, of which waited for: 2 -> 3; matrix products, arithmetic and copies ran while one was open for 1% -> 0% of each run, Pallas kernels for 0% -> 0%
where the time goes in v1:
time: 190 us
  waiting for transfers between devices  133 us (70%)
  blocking collectives  23.8 us (13%)
  between operations  15.9 us (8%)
  matrix products  9.9 us (5%)
  other arithmetic  4.2 us (2%)
  local copies, waits for them, and re-layouts  2.31 us (1%)
    psum x1, waiting for transfers between devices, per_device(): both_sums = lax.psum(partial, 'sec')  59.3 us
    all_gather x1, waiting for transfers between devices, per_device(): visit_rows = lax.all_gather(counterpart_slice, 'blk', axis=0, tiled=True)  50.5 us
    psum x1, waiting for transfers between devices, per_device(): partial = lax.psum(stacked, 'mp')  23.5 us
    unnamed x1, blocking collectives  12.1 us
    all_gather x1, blocking collectives, per_device(): both_grads = lax.all_gather(own_demb[None], 'sec', axis=0, tiled=True)  11.7 us
    dot_general x1, matrix products, per_device(): lax.dot_general(resident_slice, visit_rows, (((1,), (1,)), ((), ())), pre...  4.68 us
  transfers between devices with their start and end apart: 3, of which 3 were waited for; matrix products, arithmetic and copies ran while one was open for 0% of the time, Pallas kernels for 0%

profile of v1, /device:TPU:0, one launch (start us, length us, event | category | flops | bytes accessed | tf_op | source)
XLA Modules:
  0.0 189.5 jit_solution(14514563013629098337)
XLA Ops:
  7.2 0.0 copy-start
  7.2 0.0 copy-start.4
  7.2 0.0 copy-start.2
  7.2 0.0 all-reduce.4.cloned.1.call-start
  7.2 1.2 copy-done
  8.4 1.4 convolution_bitcast_fusion
  9.8 0.0 copy-done.4
  9.8 0.0 copy-done.2
  9.8 0.4 convolution_bitcast_fusion.1
  10.2 1.3 pad_maximum_fusion
  11.6 0.0 all-reduce.4.cloned.1.call-update
  11.6 0.0 all-reduce.6.cloned.1.call-start
  11.6 23.5 %all-reduce.4.cloned.1.call-done = f32[2,192,1152]{2,1,0:T(8,128)} async-done(((f32[2,192,1152]{2,1,0:T(8,128)}), f32[2,192,1152]{2,1,0:T(8,128)}) %all-reduce.4.cloned.1.call-update) | async-done | bytes 1769488 | tf_op jit(solution)/shard_map/psum | solution.py:25
  35.1 0.0 all-reduce.6.cloned.1.call-update
  35.1 0.0 all-gather.3.cloned.1.call-start
  35.2 59.3 %all-reduce.6.cloned.1.call-done = f32[2,192,1152]{2,1,0:T(8,128)} async-done(((f32[2,192,1152]{2,1,0:T(8,128)}), f32[2,192,1152]{2,1,0:T(8,128)}) %all-reduce.6.cloned.1.call-update) | async-done | bytes 1769488 | tf_op jit(solution)/shard_map/psum | solution.py:26
  94.5 0.0 copy-start.1
  94.5 1.8 fusion.7
  96.3 0.0 copy-start.7
  96.3 0.0 copy-start.5
  96.3 0.2 copy-done.1
  96.5 0.9 fusion.6
  97.4 0.0 all-gather.3.cloned.1.call-update
  98.8 0.0 copy-done.7
  98.8 0.6 dynamic-slice
  100.0 0.0 copy-done.5
  100.0 0.3 dynamic-update-slice
  100.3 12.1 %all-reduce = s32[1536]{0:T(1024)S(1)} all-reduce(s32[1536]{0:T(1024)S(1)} %dynamic-update-slice), channel_id=1, replica_groups=mesh['sec'=2,'blk'=8,'mp'=2] {'blk'}, use_global_device_ids=true, to_apply=%add | all-reduce | flops 1536 | bytes 12288
  112.4 50.5 %all-gather.3.cloned.1.call-done = bf16[1536,1152]{1,0:T(8,128)(2,1)} async-done(((bf16[192,1152]{1,0:T(8,128)(2,1)}), bf16[1536,1152]{1,0:T(8,128)(2,1)}) %all-gather.3.cloned.1.call-update) | async-done | bytes 3538960 | tf_op jit(solution)/shard_map/all_gather | solution.py:35
  162.9 0.0 copy-start.6
  162.9 4.7 %fusion.4 = (f32[192]{0:T(256)}, f32[192,1536]{1,0:T(8,128)S(1)}) fusion(f32[]{:T(128)} %bitcast.37, bf16[1536,1152]{1,0:T(8,128)(2,1)} %all-gather.3.cloned.1.call-done, f32[192]{0:T(256)S(1)} %add_sqrt_fusion.1, f32[2,192,1152]{2,1,0:T(8,128)S(1)} %copy-done.1, s32[]{:T(128)S(6)} %select_n.16, f32[]{:T(128)} %bitcast.1, s32[1536]{0:T(1024)S(1)} %all-reduce, ...), kind=kOutput, calls=%fused_computation.11 | convolution fusion | flops 683753280 | bytes 5614348 | tf_op jit(solution)/shard_map/dot_general | solution.py:39
  167.5 0.0 copy-done.6
  167.6 1.1 multiply_reduce_fusion
  168.7 0.2 divide_convert_fusion
  168.9 0.0 copy-start.3
  168.9 11.7 %all-gather = bf16[384,1152]{1,0:T(8,128)(2,1)S(1)} all-gather(bf16[192,1152]{1,0:T(8,128)(2,1)S(1)} %divide_convert_fusion), channel_id=2, replica_groups=mesh['sec'=2,'blk'=8,'mp'=2] {'sec'}, dimensions={0}, use_global_device_ids=true | all-gather | bytes 1327104 | tf_op jit(solution)/shard_map/all_gather | solution.py:57
  180.7 0.0 copy-done.3
  180.7 1.1 convolution_convert_fusion.1
  181.8 1.2 convolution_convert_fusion
  (3 shorter events, 0.0 us)
Async XLA Ops:
  7.2 1.3 copy-start
  7.2 2.6 %copy-start.4 = (bf16[192,384]{1,0:T(8,128)(2,1)S(1)}, bf16[192,384]{1,0:T(8,128)(2,1)}, u32[]{:S(2)}) copy-start(bf16[192,384]{1,0:T(8,128)(2,1)} %param.7) | copy-start | bytes 442372
  7.2 2.6 %copy-start.2 = (bf16[384,1152]{1,0:T(8,128)(2,1)S(1)}, bf16[384,1152]{1,0:T(8,128)(2,1)}, u32[]{:S(2)}) copy-start(bf16[384,1152]{1,0:T(8,128)(2,1)} %param.9) | copy-start | bytes 2654212
  7.2 27.9 %all-reduce.4.cloned.1.call-start = ((), (), s32[]{:S(2)}) async-start(), calls=%async_computation | async-start | bytes 3538944 | tf_op jit(solution)/shard_map/psum | solution.py:25
  11.6 82.9 %all-reduce.6.cloned.1.call-start = ((), (), s32[]{:S(2)}) async-start(), calls=%async_computation.1 | async-start | bytes 3538944 | tf_op jit(solution)/shard_map/psum | solution.py:26
  35.1 127.7 %all-gather.3.cloned.1.call-start = ((), (), s32[]{:S(2)}) async-start(), calls=%async_computation.2 | async-start | bytes 3981312 | tf_op jit(solution)/shard_map/all_gather | solution.py:35
  94.5 2.0 %copy-start.1 = (f32[2,192,1152]{2,1,0:T(8,128)S(1)}, f32[2,192,1152]{2,1,0:T(8,128)}, u32[]{:S(2)}) copy-start(f32[2,192,1152]{2,1,0:T(8,128)} %all-reduce.6.cloned.1.call-done) | copy-start | bytes 5308420
  96.3 2.5 %copy-start.7 = (u32[32]{0:T(128)S(1)}, u32[32]{0:T(128)}, u32[]{:S(2)}) copy-start(u32[32]{0:T(128)} %constant.31) | copy-start | bytes 388
  96.3 3.8 %copy-start.5 = (s32[192]{0:T(256)S(1)}, s32[192]{0:T(256)}, u32[]{:S(2)}) copy-start(s32[192]{0:T(256)} %param.13) | copy-start | bytes 2308
  162.9 4.7 %copy-start.6 = (bf16[1536,1152]{1,0:T(8,128)(2,1)S(1)}, bf16[1536,1152]{1,0:T(8,128)(2,1)}, u32[]{:S(2)}) copy-start(bf16[1536,1152]{1,0:T(8,128)(2,1)} %all-gather.3.cloned.1.call-done) | copy-start | bytes 10616836
  168.9 11.8 %copy-start.3 = (bf16[384,1152]{1,0:T(8,128)(2,1)S(1)}, bf16[384,1152]{1,0:T(8,128)(2,1)}, u32[]{:S(2)}) copy-start(bf16[384,1152]{1,0:T(8,128)(2,1)} %param.9) | copy-start | bytes 2654212
Sparse Core Ops, SparseCore 0:
  11.7 23.3 all-reduce.3
  37.5 56.9 all-reduce.5
  97.5 65.2 all-gather.2
